TPU v7x, 32 devices: a whole 2x2x4 slice. The times are simulated.
32 devices in a mesh: ctx: 8 (over z, x), head: 4 (over y, core).
Axes of the slice: x: 2, y: 2, z: 4, core: 2. Of those that a mesh axis runs over, the one named last changes fastest.
Arguments:
- hidden: bfloat16 [8192, 1536], P('ctx', 'head'), may hold values from -6 to 6
- norm_gain: float32 [1536], replicated, may hold values from 0.1 to 1.9
- zx_weight: bfloat16 [1536, 2, 3072], P(None, None, 'head'), may hold values from -0.15625 to 0.15625
- bc_weight: bfloat16 [1536, 256], replicated, may hold values from -0.15625 to 0.15625
- dt_weight: bfloat16 [1536, 48], P(None, 'head'), may hold values from -0.15625 to 0.15625
- conv_x: float32 [5, 3072], P(None, 'head'), may hold values from -0.5 to 0.5
- conv_bc: float32 [5, 256], replicated, may hold values from -0.5 to 0.5
- dt_bias: float32 [48], P('head'), may hold values from -4.6 to -2.3
- log_decay: float32 [8192, 48], P('ctx', 'head'), may hold values from -1.5 to 0, as said below
- skip_gain: float32 [48], P('head'), may hold values from 0.5 to 2
- out_gain: float32 [3072], P('head'), may hold values from 0.1 to 1.9
- out_weight: bfloat16 [3072, 1536], P('head'), may hold values from -0.109375 to 0.109375
Outputs:
- mixed: bfloat16 [8192, 1536], P('ctx', 'head')
Inputs may be any that keep to these rules, and one draw needn't show every extreme that they name: `log_decay`: negative everywhere; in some heads a token keeps only a few percent of the state after a few tens of positions, other heads decay over the whole document, and a head may lose a sizeable share of its state at single tokens.
All inputs are finite; a program needn't handle non-finite values.
Results may differ from a plain program's by a relative error of at most 0.015.
Values may be sent and summed in bfloat16 or wider, within the bound.
A program may use at most 128 MiB of HBM per device.

v0:
```python
import jax
import jax.numpy as jnp
from jax import lax
from jax.sharding import PartitionSpec as P

HEADDIM = 64
STATE = 128
CONV = 4
BLOCK = 256
INNER = 3072


eps = 1e-05


def shifted(array, axis, by):
    length = lax.axis_size(axis)
    pairs = [(i, i + by) for i in range(length) if 0 <= i + by < length]
    return lax.ppermute(array, axis, pairs)


def carried_in(array, axis, join, neutral):
    place = lax.axis_index(axis)
    gathered = jax.tree.map(
        lambda a, kind: lax.all_gather(a.astype(kind), axis), array, (jnp.bfloat16, jnp.bfloat16)
    )
    state = jax.tree.map(lambda a, e: jnp.zeros_like(a) + jnp.asarray(e, a.dtype), array, neutral)

    def one(hop, state):
        return join(
            state,
            jax.tree.map(
                lambda a, own: lax.dynamic_index_in_dim(a, hop, 0, False).astype(own.dtype),
                gathered,
                array,
            ),
        )

    return lax.fori_loop(0, place, one, state)


def project_rows(row_block, norm_gain, zx_weight, bc_weight, dt_weight):
    values = row_block.astype(jnp.float32)
    mean_square = jnp.mean(values * values, axis=-1, keepdims=True)
    normed = (values * lax.rsqrt(mean_square + eps) * norm_gain).astype(jnp.bfloat16)
    flat_weight = zx_weight.reshape(zx_weight.shape[0], -1)
    gate_and_x = jnp.dot(normed, flat_weight, preferred_element_type=jnp.float32).astype(
        jnp.bfloat16
    )
    b_and_c = jnp.dot(normed, bc_weight, preferred_element_type=jnp.float32).astype(jnp.bfloat16)
    step_raw = jnp.dot(normed, dt_weight, preferred_element_type=jnp.float32).astype(jnp.bfloat16)
    return (gate_and_x, b_and_c, step_raw)


def convolve(extended, conv_taps):
    tap_count = conv_taps.shape[0] - 1
    out_rows = extended.shape[0] - tap_count + 1
    summed_taps = conv_taps[tap_count]
    for offset in range(tap_count):
        summed_taps = summed_taps + conv_taps[offset] * extended[offset : offset + out_rows].astype(
            jnp.float32
        )
    return jax.nn.silu(summed_taps).astype(jnp.bfloat16)


def combine(earlier_pair, later_pair):
    return (
        earlier_pair[0] + later_pair[0],
        jnp.exp(later_pair[0])[:, None, None] * earlier_pair[1] + later_pair[1],
    )


def per_device(
    hidden,
    norm_gain,
    zx_weight,
    bc_weight,
    dt_weight,
    conv_x,
    conv_bc,
    dt_bias,
    log_decay,
    skip_gain,
    out_gain,
    out_weight,
):
    row_count = hidden.shape[0]
    heads_here = dt_weight.shape[1]
    inner_here = zx_weight.shape[2]
    rim_rows = CONV - 1
    highest = lax.Precision.HIGHEST
    gathered = lax.all_gather(hidden, "head", axis=1, tiled=True)
    gate_and_x, b_and_c, step_raw = project_rows(
        gathered, norm_gain, zx_weight, bc_weight, dt_weight
    )
    x_proj = gate_and_x[:, inner_here:]
    x_before, bc_before = shifted(
        (x_proj[row_count - rim_rows :], b_and_c[row_count - rim_rows :]), "ctx", 1
    )
    x_extended = jnp.concatenate([x_before, x_proj], axis=0)
    bc_extended = jnp.concatenate([bc_before, b_and_c], axis=0)
    gate_raw = gate_and_x[:, :inner_here]
    x_conv = convolve(x_extended, conv_x)
    bc_conv = convolve(bc_extended, conv_bc)
    step_size = jax.nn.softplus(step_raw.astype(jnp.float32) + dt_bias)
    block_count = row_count // BLOCK
    x_heads = x_conv.reshape(block_count, BLOCK, heads_here, HEADDIM)
    b_blocks = bc_conv[:, :STATE].reshape(block_count, BLOCK, STATE)
    c_blocks = bc_conv[:, STATE:].reshape(block_count, BLOCK, STATE)
    decay_sum = jnp.cumsum(log_decay.reshape(block_count, BLOCK, heads_here), axis=1)
    decay_t = jnp.transpose(decay_sum, (0, 2, 1))
    step_t = jnp.transpose(step_size.reshape(block_count, BLOCK, heads_here), (0, 2, 1))
    scores = jnp.einsum("ctn,csn->cts", c_blocks, b_blocks, preferred_element_type=jnp.float32)
    position = jnp.arange(BLOCK)
    causal = position[:, None] >= position[None, :]
    log_gap = jnp.where(causal, decay_t[:, :, :, None] - decay_t[:, :, None, :], 0.0)
    mix_weights = jnp.where(
        causal, scores[:, None] * jnp.exp(log_gap) * step_t[:, :, None, :], 0.0
    ).astype(jnp.bfloat16)
    y_inside = jnp.einsum(
        "chts,cshp->cthp", mix_weights, x_heads, preferred_element_type=jnp.float32
    )
    to_end = jnp.exp(decay_t[:, :, -1:] - decay_t) * step_t
    x_wide = x_heads.astype(jnp.float32)
    weighted = x_wide * jnp.transpose(to_end, (0, 2, 1))[..., None]
    b_wide = b_blocks.astype(jnp.float32)
    c_wide = c_blocks.astype(jnp.float32)
    states = jnp.einsum("cshp,csn->chpn", weighted, b_wide, precision=highest)
    totals = decay_t[:, :, -1]
    entering = []
    running = jnp.zeros_like(states[0])
    for index in range(block_count):
        entering.append(running)
        running = jnp.exp(totals[index])[:, None, None] * running + states[index]
    entering = jnp.stack(entering)
    before = jnp.concatenate([jnp.zeros_like(totals[:1]), jnp.cumsum(totals, axis=0)[:-1]], axis=0)
    scanned = carried_in(
        (jnp.sum(totals, axis=0), running),
        "ctx",
        combine,
        (jnp.zeros_like(totals[0]), jnp.zeros_like(running)),
    )
    incoming = scanned[1]
    decay_gain = jnp.exp(decay_sum)[..., None]
    carried = entering + jnp.exp(before)[:, :, None, None] * incoming[None]
    y_carried = decay_gain * jnp.einsum("ctn,chpn->cthp", c_wide, carried, precision=highest)
    y_heads = y_inside + y_carried + skip_gain[:, None] * x_wide
    gated = y_heads.reshape(row_count, inner_here) * jax.nn.silu(gate_raw.astype(jnp.float32))
    square_sum = lax.psum(jnp.sum(gated * gated, axis=-1), "head")
    y_normed = (gated * lax.rsqrt(square_sum / INNER + eps)[:, None] * out_gain).astype(
        jnp.bfloat16
    )
    partial_value = jnp.dot(y_normed, out_weight, preferred_element_type=jnp.float32)
    return lax.psum_scatter(
        partial_value.astype(jnp.bfloat16), "head", scatter_dimension=1, tiled=True
    )


def solution(mesh):
    placed = (
        P("ctx", "head"),
        P(),
        P(None, None, "head"),
        P(),
        P(None, "head"),
        P(None, "head"),
        P(),
        P("head"),
        P("ctx", "head"),
        P("head"),
        P("head"),
        P("head", None),
    )
    return jax.shard_map(
        per_device, mesh=mesh, in_specs=placed, out_specs=P("ctx", "head"), check_vma=False
    )
```

profile of v0, /device:TPU:24, one launch (start us, length us, event | category | flops | bytes accessed | tf_op | source)
XLA Modules:
  0.0 207.8 jit_solution(3511831182408516563)
XLA Ops:
  7.3 5.4 %copy.76 = bf16[192,8,2,768]{3,1,2,0:T(8,128)(2,1)} copy(bf16[192,8,2,768]{3,2,1,0:T(2,128)(2,1)} %bitcast.72) | data formatting | bytes 9437184
  12.9 2.3 %reduce-window.6 = f32[4,12,2,128]{3,1,2,0:T(8,128)S(1)} reduce-window(f32[4,12,2,128]{3,1,2,0:T(8,128)S(1)} %copy.57, f32[]{:T(128)} %constant.44.clone.1), window={size=1x1x1x128 pad=0_0x0_0x0_0x127_0}, to_apply=%region_1.2 | reduce-window | flops 1560576 | bytes 98308 | tf_op jit(solution)/shard_map/reduce-window
  16.4 21.9 %all-gather.4.cloned.1.call-done = bf16[1024,1536]{1,0:T(8,128)(2,1)} async-done(((bf16[1024,384]{1,0:T(8,128)(2,1)}), bf16[1024,1536]{1,0:T(8,128)(2,1)}) %all-gather.4.cloned.1.call-update) | async-done | bytes 3145744 | tf_op jit(solution)/shard_map/all_gather | solution.py:92
  38.4 2.7 %fusion.1 = f32[1024]{0:T(1024)S(1)} fusion(bf16[1024,1536]{1,0:T(8,128)(2,1)} %all-gather.4.cloned.1.call-done), kind=kLoop, calls=%fused_computation.6 | loop fusion | flops 4717568 | bytes 3149824 | tf_op jit(solution)/shard_map/reduce_sum | solution.py:44
  41.2 7.8 %convolution_convert_fusion.1 = bf16[1024,1536]{1,0:T(8,128)(2,1)S(1)} fusion(bf16[1536,1536]{1,0:T(8,128)(2,1)} %bitcast.73, bf16[1024,1536]{1,0:T(8,128)(2,1)S(1)} %copy-done.3, f32[1536]{0:T(1024)S(1)} %copy-done.13, f32[1024]{0:T(1024)S(1)} %add_rsqrt_fusion.1), kind=kOutput, calls=%fused_computation.20 | convolution fusion | flops 4839702528 | bytes 11020288 | tf_op jit(solution)/shard_map/dot_general | solution.py:47
  49.1 3.6 %collective-permute-start = (bf16[3,768]{1,0:T(4,128)(2,1)S(1)}, bf16[3,768]{1,0:T(4,128)(2,1)S(1)}, u32[]{:S(2)}, u32[]{:S(2)}) collective-permute-start(bf16[3,768]{1,0:T(4,128)(2,1)S(1)} %slice.146), channel_id=1, source_target_pairs={{0,4},{4,8},{8,12},{12,16},{16,20},{20,24},{24,28},{1,5},{5,9},{9,... | collective-permute-start | bytes 13832 | tf_op jit(solution)/shard_map/ppermute | solution.py:19
  53.8 1.9 collective-permute-start.1
  57.0 3.2 %collective-permute-done.1 = bf16[3,256]{1,0:T(4,128)(2,1)S(1)} collective-permute-done((bf16[3,256]{1,0:T(4,128)(2,1)S(1)}, bf16[3,256]{1,0:T(4,128)(2,1)S(1)}, u32[]{:S(2)}, u32[]{:S(2)}) %collective-permute-start.1) | collective-permute-done | bytes 1568 | tf_op jit(solution)/shard_map/ppermute | solution.py:19
  61.0 3.2 %multiply_convert_fusion.1 = bf16[1024,768]{1,0:T(8,128)(2,1)} fusion(bf16[1024,768]{1,0:T(8,128)(2,1)S(1)} %slice-done, bf16[3,768]{1,0:T(4,128)(2,1)S(1)} %collective-permute-done, f32[768]{0:T(1024)S(1)} %get-tuple-element.57, f32[768]{0:T(1024)S(1)} %get-tuple-element.58, f32[768]{0:T(1024)S(1)} %get-tuple-element.55, f32[768]{0:T(1024)S(1)} %get-tuple-element.56, ...), kind=kLoop, calls=%fused_computation.30 | loop fusion | flops 20447232 | bytes 3165696 | tf_op jit(solution)/shard_map/convert_element_type | solution.py:63
  64.2 2.6 %copy.56 = bf16[1024,768]{0,1:T(8,128)(2,1)} copy(bf16[1024,768]{1,0:T(8,128)(2,1)} %multiply_convert_fusion.1) | data formatting | bytes 3145728 | tf_op jit(solution)/shard_map/convert_element_type | solution.py:63
  66.8 3.9 %reshape.124 = bf16[4,256,12,64]{1,0,3,2:T(4,128)(2,1)} reshape(bf16[1024,768]{0,1:T(8,128)(2,1)} %copy.56) | data formatting | bytes 3145728 | tf_op jit(solution)/shard_map/reshape | solution.py:107
  70.6 3.2 %fusion.10 = f32[4,12,64,128]{3,2,1,0:T(8,128)S(1)} fusion(bf16[4,256,128,1]{2,1,3,0:T(8,128)(2,1)S(1)} %bitcast.76, f32[4,256,12]{1,2,0:T(8,128)S(1)} %copy.69, bf16[4,256,12,64]{1,0,3,2:T(4,128)(2,1)} %reshape.124), kind=kOutput, calls=%fused_computation.21 | convolution fusion | flops 1209532416 | bytes 3457024 | tf_op jit(solution)/shard_map/cshp,csn->chpn/dot_general | solution.py:128
  77.0 14.6 %all-reduce.1 = bf16[96]{0:T(256)(128)(2,1)S(1)} all-reduce(bf16[96]{0:T(256)(128)(2,1)S(1)} %dynamic-update-slice), channel_id=2, replica_groups=mesh['ctx'=8,'head'=4] {'ctx'}, use_global_device_ids=true, to_apply=%add.1 | all-reduce | flops 96 | bytes 384
  93.0 1.3 fusion.53
  94.3 22.5 %all-gather.6.cloned.1.call-done = bf16[8,12,64,128]{3,2,1,0:T(8,128)(2,1)} async-done(((bf16[1,12,64,128]{3,2,1,0:T(8,128)(2,1)}), bf16[8,12,64,128]{3,2,1,0:T(8,128)(2,1)}) %all-gather.6.cloned.1.call-update) | async-done | bytes 1572880 | tf_op jit(solution)/shard_map/all_gather | solution.py:25
  116.9 6.7 %while.12 = (s32[]{:T(128)}, f32[12,64,128]{2,1,0:T(8,128)S(1)}, s32[]{:T(128)}, bf16[8,12]{1,0:T(8,128)(2,1)S(1)}, bf16[8,12,64,128]{3,2,1,0:T(8,128)(2,1)}, /*index=5*/s32[]{:T(128)}, s32[]{:T(128)}, s32[]{:T(128)}) while((s32[]{:T(128)}, f32[12,64,128]{2,1,0:T(8,128)S(1)}, s32[]{:T(128)}, bf16[8,12]{1,0:T(8,128)(2,1)S(1)}, ...), condition=%wide.region_6.7_spmd, body=%wide.region_5.6_spmd.sunk | while | flops 294929 | bytes 983287 | solution.py:39
  116.9 1.1 convert_add_fusion.2
  118.0 1.1 convert_add_fusion.2
  119.1 1.1 convert_add_fusion.2
  121.4 1.1 convert_add_fusion.2
  122.5 1.1 convert_add_fusion.2
  123.6 2.7 %fusion.18 = f32[4,256,12,64]{1,3,2,0:T(8,128)S(1)} fusion(bf16[4,256,128,1]{2,1,3,0:T(8,128)(2,1)S(1)} %bitcast.75, f32[1,12,64,128]{3,2,1,0:T(8,128)S(1)} %get-tuple-element.70, f32[1,12,64,128]{3,2,1,0:T(8,128)} %get-tuple-element.71, f32[1,12,64,128]{3,2,1,0:T(8,128)} %get-tuple-element.72, f32[4]{0:T(128)S(1)} %pad.1.clone, ...), kind=kOutput, calls=%fused_computation.37 | convolution fusion | flops 1209925632 | bytes 4980944 | tf_op jit(solution)/shard_map/ctn,chpn->cthp/dot_general | solution.py:146
  126.4 4.0 %fusion.11 = f32[4,256,12,64]{1,3,2,0:T(8,128)S(1)} fusion(f32[4,256,12,64]{1,3,2,0:T(8,128)S(1)} %fusion.18, f32[4,12,256]{2,1,0:T(8,128)S(1)} %copy.63, f32[4,12,256]{2,1,0:T(8,128)S(1)} %copy-done.6, f32[4,256,256]{2,1,0:T(8,128)S(1)} %copy-done.4, pred[256,256]{1,0:T(8,128)(4,1)S(1)} %copy-done.8, f32[12]{0:T(128)S(1)} %copy-done.16, ...), kind=kOutput, calls=%fused_computation.22 | convolution fusion | flops 425459712 | bytes 9125936 | tf_op jit(solution)/shard_map/chts,cshp->cthp/dot_general | solution.py:120
  130.3 2.0 copy.70
  132.4 2.4 %copy.77 = f32[96,8,4,256]{3,1,2,0:T(8,128)} copy(f32[96,8,4,256]{3,2,1,0:T(4,128)S(1)} %bitcast.70) | data formatting | bytes 6291456
  134.8 3.6 %copy.71 = f32[1024,768]{1,0:T(8,128)} copy(f32[1024,768]{0,1:T(8,128)} %bitcast.71) | data formatting | bytes 6291456 | tf_op jit(solution)/shard_map/reshape | solution.py:148
  138.4 3.5 %multiply_reduce_fusion = f32[1024]{0:T(1024)S(1)} fusion(f32[1024,768]{1,0:T(8,128)} %copy.71, bf16[1024,1536]{1,0:T(8,128)(2,1)} %copy-done.2), kind=kLoop, calls=%fused_computation.29 | loop fusion | flops 6290432 | bytes 4722688 | tf_op jit(solution)/shard_map/reduce_sum | solution.py:149
  141.9 6.0 %psum.7 = f32[1024]{0:T(1024)S(1)} all-reduce(f32[1024]{0:T(1024)S(1)} %multiply_reduce_fusion), channel_id=1, replica_groups=mesh['ctx'=8,'head'=4] {'head'}, use_global_device_ids=true, to_apply=%region_8.9 | all-reduce | flops 1024 | bytes 8192 | tf_op jit(solution)/shard_map/psum | solution.py:149
  148.0 7.3 %convolution_convert_fusion = bf16[1024,1536]{1,0:T(8,128)(2,1)} fusion(bf16[768,1536]{1,0:T(8,128)(2,1)S(1)} %copy-done, f32[768]{0:T(1024)S(1)} %copy-done.14, f32[1024]{0:T(1024)S(1)} %add_rsqrt_fusion, f32[1024,768]{1,0:T(8,128)} %copy.71, bf16[1024,1536]{1,0:T(8,128)(2,1)} %copy-done.2), kind=kOutput, calls=%fused_computation.19 | convolution fusion | flops 2424569856 | bytes 10230784 | tf_op jit(solution)/shard_map/dot_general | solution.py:153
  155.3 4.6 %copy.74 = bf16[1024,1536]{0,1:T(8,128)(2,1)} copy(bf16[1024,1536]{1,0:T(8,128)(2,1)} %convolution_convert_fusion) | data formatting | bytes 6291456
  159.9 39.0 %reduce-scatter.4.cloned.1.call-done = bf16[384,1024]{1,0:T(8,128)(2,1)} async-done(((bf16[1536,1024]{1,0:T(8,128)(2,1)}), bf16[384,1024]{1,0:T(8,128)(2,1)}) %reduce-scatter.4.cloned.1.call-update) | async-done | bytes 786448
  199.0 2.3 %copy.75 = bf16[1024,384]{1,0:T(8,128)(2,1)} copy(bf16[1024,384]{0,1:T(8,128)(2,1)} %bitcast.78) | data formatting | bytes 1572864
  (93 shorter events, 10.4 us)
Async XLA Ops:
  6.5 141.4 %copy-start = (bf16[768,1536]{1,0:T(8,128)(2,1)S(1)}, bf16[768,1536]{1,0:T(8,128)(2,1)}, u32[]{:S(2)}) copy-start(bf16[768,1536]{1,0:T(8,128)(2,1)} %param.25) | copy-start | bytes 7077892
  6.5 31.8 %all-gather.4.cloned.1.call-start = ((), (), s32[]{:S(2)}) async-start(), calls=%async_computation.1 | async-start | bytes 3932160 | tf_op jit(solution)/shard_map/all_gather | solution.py:92
  7.3 109.6 %all-gather.6.cloned.1.call-start = ((), (), s32[]{:S(2)}) async-start(), calls=%async_computation.2 | async-start | bytes 1769472 | tf_op jit(solution)/shard_map/all_gather | solution.py:25
  7.3 5.5 %copy-start.5 = (f32[1024,12]{0,1:T(8,128)S(1)}, f32[1024,12]{0,1:T(8,128)}, u32[]{:S(2)}) copy-start(f32[1024,12]{0,1:T(8,128)} %param.22) | copy-start | bytes 147460
  7.3 8.7 %copy-start.9 = (f32[5,768]{1,0:T(8,128)S(1)}, f32[5,768]{1,0:T(8,128)}, u32[]{:S(2)}) copy-start(f32[5,768]{1,0:T(8,128)} %param.19) | copy-start | bytes 46084
  7.3 9.1 %copy-start.10 = (f32[5,256]{1,0:T(8,128)S(1)}, f32[5,256]{1,0:T(8,128)}, u32[]{:S(2)}) copy-start(f32[5,256]{1,0:T(8,128)} %param.20) | copy-start | bytes 15364
  12.8 28.3 %copy-start.13 = (f32[1536]{0:T(1024)S(1)}, f32[1536]{0:T(1024)}, u32[]{:S(2)}) copy-start(f32[1536]{0:T(1024)} %param.15) | copy-start | bytes 18436
  38.4 2.8 %copy-start.3 = (bf16[1024,1536]{1,0:T(8,128)(2,1)S(1)}, bf16[1024,1536]{1,0:T(8,128)(2,1)}, u32[]{:S(2)}) copy-start(bf16[1024,1536]{1,0:T(8,128)(2,1)} %all-gather.4.cloned.1.call-done) | copy-start | bytes 9437188
  49.1 4.7 %copy-start.2 = (bf16[1024,1536]{1,0:T(8,128)(2,1)}, bf16[1024,1536]{1,0:T(8,128)(2,1)S(1)}, u32[]{:S(2)}) copy-start(bf16[1024,1536]{1,0:T(8,128)(2,1)S(1)} %convolution_convert_fusion.1) | copy-start | bytes 9437188
  49.1 3.7 %copy-start.11 = (bf16[1536,256]{1,0:T(8,128)(2,1)S(1)}, bf16[1536,256]{1,0:T(8,128)(2,1)}, u32[]{:S(2)}) copy-start(bf16[1536,256]{1,0:T(8,128)(2,1)} %param.17) | copy-start | bytes 2359300
  49.1 6.7 %copy-start.12 = (bf16[1536,12]{0,1:T(8,128)(2,1)S(1)}, bf16[1536,12]{0,1:T(8,128)(2,1)}, u32[]{:S(2)}) copy-start(bf16[1536,12]{0,1:T(8,128)(2,1)} %param.18) | copy-start | bytes 110596
  49.1 6.7 %copy-start.15 = (f32[12]{0:T(128)S(1)}, f32[12]{0:T(128)}, u32[]{:S(2)}) copy-start(f32[12]{0:T(128)} %param.21) | copy-start | bytes 148
  49.1 11.8 %collective-permute-start = (bf16[3,768]{1,0:T(4,128)(2,1)S(1)}, bf16[3,768]{1,0:T(4,128)(2,1)S(1)}, u32[]{:S(2)}, u32[]{:S(2)}) collective-permute-start(bf16[3,768]{1,0:T(4,128)(2,1)S(1)} %slice.146), channel_id=1, source_target_pairs={{0,4},{4,8},{8,12},{12,16},{16,20},{20,24},{24,28},{1,5},{5,9},{9,... | collective-permute-start | bytes 13832 | tf_op jit(solution)/shard_map/ppermute | solution.py:19
  53.8 6.4 %collective-permute-start.1 = (bf16[3,256]{1,0:T(4,128)(2,1)S(1)}, bf16[3,256]{1,0:T(4,128)(2,1)S(1)}, u32[]{:S(2)}, u32[]{:S(2)}) collective-permute-start(bf16[3,256]{1,0:T(4,128)(2,1)S(1)} %slice.152), channel_id=1, source_target_pairs={{0,4},{4,8},{8,12},{12,16},{16,20},{20,24},{24,28},{1,5},{5,9},{9,... | collective-permute-start | bytes 4616 | tf_op jit(solution)/shard_map/ppermute | solution.py:19
  56.8 4.1 %slice-start = ((bf16[1024,1536]{1,0:T(8,128)(2,1)}), bf16[1024,768]{1,0:T(8,128)(2,1)S(1)}, s32[]{:S(2)}) async-start(bf16[1024,1536]{1,0:T(8,128)(2,1)} %copy-done.2), calls=%async_computation.4 | async-start | bytes 3145728 | tf_op jit(solution)/shard_map/slice | solution.py:96
  70.6 5.0 %copy-start.17 = (u32[32]{0:T(128)S(1)}, u32[32]{0:T(128)}, u32[]{:S(2)}) copy-start(u32[32]{0:T(128)} %constant.56) | copy-start | bytes 388
  74.9 124.1 %reduce-scatter.4.cloned.1.call-start = ((), (), s32[]{:S(2)}) async-start(), calls=%async_computation.3 | async-start | bytes 3932160
  123.6 2.8 %copy-start.1 = (bf16[4,256,12,64]{1,0,3,2:T(4,128)(2,1)S(1)}, bf16[4,256,12,64]{1,0,3,2:T(4,128)(2,1)}, u32[]{:S(2)}) copy-start(bf16[4,256,12,64]{1,0,3,2:T(4,128)(2,1)} %reshape.124) | copy-start | bytes 4718596
  123.6 2.8 %copy-start.4 = (f32[4,256,256]{2,1,0:T(8,128)S(1)}, f32[4,256,256]{2,1,0:T(8,128)}, u32[]{:S(2)}) copy-start(f32[4,256,256]{2,1,0:T(8,128)} %fusion.53) | copy-start | bytes 3145732
  123.6 2.8 %copy-start.6 = (f32[4,12,256]{2,1,0:T(8,128)S(1)}, f32[4,12,256]{2,1,0:T(8,128)}, u32[]{:S(2)}) copy-start(f32[4,12,256]{2,1,0:T(8,128)} %copy.61) | copy-start | bytes 147460
  123.6 2.8 %copy-start.7 = (f32[4,256,12]{1,2,0:T(8,128)S(1)}, f32[4,256,12]{1,2,0:T(8,128)}, u32[]{:S(2)}) copy-start(f32[4,256,12]{1,2,0:T(8,128)} %copy.65) | copy-start | bytes 147460
  123.6 2.8 %copy-start.8 = (pred[256,256]{1,0:T(8,128)(4,1)S(1)}, pred[256,256]{1,0:T(8,128)(4,1)}, u32[]{:S(2)}) copy-start(pred[256,256]{1,0:T(8,128)(4,1)} %iota_compare_fusion) | copy-start | bytes 196612
  123.6 2.8 %copy-start.16 = (f32[12]{0:T(128)S(1)}, f32[12]{0:T(128)}, u32[]{:S(2)}) copy-start(f32[12]{0:T(128)} %param.23) | copy-start | bytes 148
  138.4 9.5 %copy-start.14 = (f32[768]{0:T(1024)S(1)}, f32[768]{0:T(1024)}, u32[]{:S(2)}) copy-start(f32[768]{0:T(1024)} %param.24) | copy-start | bytes 9220
Sparse Core Ops, SparseCore 0:
  8.9 29.4 all-gather.3
  75.0 41.7 all-gather.5
  160.0 38.8 reduce-scatter.3
where the time goes:
time: 210 us; the launch traced here: 208 us
  waiting for transfers between devices  87.4 us (42%)
  local copies, waits for them, and re-layouts  30 us (14%)
  matrix products  28.3 us (13%)
  other arithmetic  21.4 us (10%)
  blocking collectives  20.7 us (10%)
  between operations  14.1 us (7%)
  starting transfers between devices  5.62 us (3%)
    unnamed x4, waiting for transfers between devices  39.8 us
    all_gather x1, waiting for transfers between devices, carried_in(): lax.all_gather(a.astype(kind), axis)  22.5 us
    all_gather x1, waiting for transfers between devices, per_device(): gathered = lax.all_gather(hidden, 'head', axis=1, tiled=True)  21.9 us
    unnamed x43, local copies, waits for them, and re-layouts  15.8 us
    unnamed x1, blocking collectives  14.6 us
    dot_general x1, matrix products, project_rows(): jnp.dot(normed, flat_weight, preferred_element_type=jnp.float32)  7.83 us
    dot_general x1, matrix products, per_device(): jnp.dot(y_normed, out_weight, preferred_element_type=jnp.float32)  7.3 us
    add x6, other arithmetic, combine(): jnp.exp(later_pair[0])[:, None, None] * earlier_pair[1] + later_pair[1]  6.4 us
  transfers between devices with their start and end apart: 5, of which 4 were waited for; matrix products, arithmetic and copies ran while one was open for 8% of the time, Pallas kernels for 0%

commit v1 on v0

v1 whole, which is shorter than its diff:
```python
import functools

import jax
import jax.numpy as jnp
from jax import lax
from jax.experimental import pallas as pl
from jax.experimental.pallas import tpu as pltpu
from jax.sharding import PartitionSpec as P

HEADDIM = 64
STATE = 128
CONV = 4
BLOCK = 256
HALO = 16
QUAD = 256
PER = QUAD // HEADDIM

eps = 1e-05
F32 = jnp.float32
BF16 = jnp.bfloat16


def dot(a, b):
    return jnp.dot(a, b, preferred_element_type=F32)


def silu(v):
    return v / (1.0 + jnp.exp(-v))


def spread(column_of, first, lane, rows):
    out = None
    for k in range(PER):
        piece = jnp.broadcast_to(column_of(first + k), (rows, QUAD))
        out = piece if out is None else jnp.where(lane >= k * HEADDIM, piece, out)
    return out


def kernel(
    places,
    hidden,
    wzx_hbm,
    wbc_hbm,
    wout_hbm,
    gain,
    wdt_in,
    taps_x,
    taps_bc,
    dtb,
    ld_in,
    skip,
    out_gain,
    out,
    xg,
    wzx,
    wbc,
    wout,
    wdt,
    nrm,
    tail,
    ldp,
    gate,
    xc,
    cm,
    yi,
    ent,
    tl,
    ed,
    st,
    dsum,
    got_s,
    got_d,
    snd_s,
    snd_d,
    got_e,
    snd_e,
    back,
    inc,
    gb,
    send_p,
    recv_p,
    own,
    send_y,
    recv_y,
    sq,
    load_sem,
    ys,
    yr,
    ps,
    pr,
    fs,
    fr,
    hs,
    hr,
    cs,
    cr,
    es,
    er,
    bs,
    br,
    rs,
    rr,
    zs,
    zr,
    qs,
    qr,
):
    places_ctx = places
    rows, feat = hidden.shape
    width = 4 * feat
    inner = wzx.shape[1] // 2
    heads = inner // HEADDIM
    quads = inner // QUAD
    chunks = rows // BLOCK
    ctx = lax.axis_index("ctx")
    me = lax.axis_index("head")
    partner = me + 1 - 2 * lax.rem(me, 2)
    other = lax.rem(me + 2, 4)
    diag = lax.rem(partner + 2, 4)
    odd = lax.rem(ctx, 2)
    MESH = pl.DeviceIdType.MESH

    def remote(src, dst, ss, rsem, c, h):
        return pltpu.make_async_remote_copy(
            src_ref=src, dst_ref=dst, send_sem=ss, recv_sem=rsem, device_id=(c, h), device_id_type=MESH
        )

    own_load = pltpu.make_async_copy(hidden, xg.at[me, pl.ds(HALO, rows)], load_sem.at[0])
    loads = [
        pltpu.make_async_copy(wbc_hbm, wbc, load_sem.at[1]),
        pltpu.make_async_copy(wzx_hbm, wzx, load_sem.at[2]),
    ]
    out_load = pltpu.make_async_copy(wout_hbm, wout, load_sem.at[3])

    barrier = pltpu.get_barrier_semaphore()

    def greet(c, h):
        pl.semaphore_signal(barrier, inc=1, device_id=(c, h), device_id_type=MESH)

    for h in (partner, other, diag):
        greet(ctx, h)

    @pl.when(ctx > 0)
    def _():
        for h in range(4):
            greet(ctx - 1, h)

    @pl.when(ctx < places_ctx - 1)
    def _():
        for h in range(4):
            greet(ctx + 1, h)

    @pl.when(ctx >= 2)
    def _():
        greet(ctx - 2, me)

    @pl.when(ctx < places_ctx - 2)
    def _():
        greet(ctx + 2, me)

    own_load.start()
    for load in loads:
        load.start()
    out_load.start()
    below = lax.div(ctx + places_ctx - 1, places_ctx)
    above = lax.div(2 * places_ctx - 2 - ctx, places_ctx)
    two_below = lax.div(ctx + places_ctx - 2, places_ctx)
    two_above = lax.div(2 * places_ctx - 3 - ctx, places_ctx)
    pl.semaphore_wait(barrier, 3 + 4 * (below + above) + two_below + two_above)

    def src_rows(c):
        return hidden.at[pl.ds(pl.multiple_of(c * BLOCK, BLOCK), BLOCK)]

    def slot(h, c):
        return xg.at[h, pl.ds(pl.multiple_of(HALO + c * BLOCK, HALO), BLOCK)]

    def to_y(c):
        return remote(src_rows(c), slot(me, c), ys.at[c], yr.at[c], ctx, other)

    def to_p(c):
        return remote(src_rows(c), slot(me, c), ps.at[c], pr.at[c], ctx, partner)

    def forward(c):
        return remote(slot(other, c), slot(other, c), fs.at[c], fr.at[c], ctx, partner)

    def halo(h, sender):
        return remote(
            hidden.at[pl.ds(rows - HALO, HALO)],
            xg.at[sender, pl.ds(0, HALO)],
            hs.at[h],
            hr.at[sender],
            ctx + 1,
            h,
        )

    @pl.when(ctx < places_ctx - 1)
    def _():
        for h in range(4):
            halo(h, me).start()

    for c in range(chunks):
        to_y(c).start()
    for c in range(chunks):
        to_p(c).start()

    @pl.when(ctx == 0)
    def _():
        xg[:, 0:HALO, :] = jnp.zeros((4, HALO, feat), BF16)

    wdt[...] = jnp.zeros_like(wdt)
    wdt[:, 0:heads] = wdt_in[...]
    ldp[...] = jnp.zeros_like(ldp)
    st[...] = jnp.zeros_like(st)
    dsum[...] = jnp.zeros_like(dsum)

    @pl.when(ctx > 0)
    def _():
        for h in range(4):
            halo(0, h).wait_recv()

    for load in loads:
        load.wait()
    own_load.wait()

    def normalised(at, count):
        vals = [xg[j, at, :].astype(F32) for j in range(4)]
        total = sum(jnp.sum(v * v, axis=-1, keepdims=True) for v in vals)
        scale = lax.rsqrt(total / width + eps)
        for j in range(4):
            span = slice(j * feat, (j + 1) * feat)
            nrm[0:count, span] = (vals[j] * scale * gain[:, span]).astype(BF16)

    normalised(pl.ds(0, HALO), HALO)
    head_rows = nrm[0:HALO, :]
    for s in range(quads):
        tail[:, s * QUAD : (s + 1) * QUAD] = dot(
            head_rows, wzx[:, inner + s * QUAD : inner + (s + 1) * QUAD]
        )
    tail[:, inner : inner + 2 * STATE] = dot(head_rows, wbc[...])

    lane = lax.broadcasted_iota(jnp.int32, (1, QUAD), 1)
    row_id = lax.broadcasted_iota(jnp.int32, (BLOCK, BLOCK), 0)
    col_id = lax.broadcasted_iota(jnp.int32, (BLOCK, BLOCK), 1)

    def convolved(raw, span, taps):
        ext = jnp.concatenate([tail[:, span], raw], axis=0)
        summed = taps[CONV : CONV + 1, :] + taps[CONV - 1 : CONV, :] * ext
        for back_by in range(1, CONV):
            at = CONV - 1 - back_by
            summed = summed + taps[at : at + 1, :] * pltpu.roll(ext, back_by, 0)
        tail[:, span] = raw[BLOCK - HALO :, :]
        return silu(summed[HALO:, :])

    def first(c, carry):
        to_y(c).wait_recv()
        forward(c).start()
        to_p(c).wait_recv()
        remote(slot(diag, c), slot(diag, c), fs.at[c], fr.at[c], ctx, partner).wait_recv()
        here = pl.ds(pl.multiple_of(c * BLOCK, BLOCK), BLOCK)
        normalised(pl.ds(pl.multiple_of(HALO + c * BLOCK, HALO), BLOCK), BLOCK)
        normed = nrm[...]
        bc = convolved(dot(normed, wbc[...]), slice(inner, inner + 2 * STATE), taps_bc[...])
        b = bc[:, :STATE].astype(BF16)
        cc = bc[:, STATE:].astype(BF16)
        cm[here, :] = cc
        raw_step = dot(normed, wdt[...]) + dtb[...]
        step = jnp.maximum(raw_step, 0.0) + jnp.log1p(jnp.exp(-jnp.abs(raw_step)))
        ldp[:, 0:heads] = ld_in[here, :]
        tri = jnp.where(row_id >= col_id, 1.0, 0.0).astype(F32)
        dcol = jnp.dot(tri, ldp[...], preferred_element_type=F32, precision=lax.Precision.HIGHEST)
        ed[here, :] = jnp.exp(dcol)
        drow = dcol.T
        srow = step.T
        wrow = jnp.exp(drow[:, BLOCK - 1 : BLOCK] - drow) * srow
        scores = lax.dot_general(
            cc, b, (((1,), (1,)), ((), ())), preferred_element_type=F32
        )
        scores = jnp.where(row_id >= col_id, scores, 0.0)
        b_t = b.astype(F32).T
        for q in range(quads):
            span = slice(q * QUAD, (q + 1) * QUAD)
            gate[here, span] = dot(normed, wzx[:, span]).astype(BF16)
            raw = dot(normed, wzx[:, inner + q * QUAD : inner + (q + 1) * QUAD])
            xq = convolved(raw, span, taps_x[:, span]).astype(BF16)
            xc[here, span] = xq
            y_acc = None
            s_acc = None
            for k in range(PER):
                h = q * PER + k
                gap = jnp.minimum(dcol[:, h : h + 1] - drow[h : h + 1, :], 0.0)
                mix = (scores * jnp.exp(gap) * srow[h : h + 1, :]).astype(BF16)
                wb = (b_t * wrow[h : h + 1, :]).astype(BF16)
                y_h = dot(mix, xq)
                s_h = dot(wb, xq)
                if k == 0:
                    y_acc, s_acc = y_h, s_h
                else:
                    y_acc = jnp.where(lane >= k * HEADDIM, y_h, y_acc)
                    s_acc = jnp.where(lane >= k * HEADDIM, s_h, s_acc)
            yi[here, span] = y_acc
            total = spread(lambda i: dcol[BLOCK - 1 : BLOCK, i : i + 1], q * PER, lane, 1)
            ent[c, :, span] = st[:, span].astype(BF16)
            tl[c, :, span] = dsum[:, span]
            st[:, span] = jnp.exp(total) * st[:, span] + s_acc
            dsum[:, span] = dsum[:, span] + total
        return carry

    lax.fori_loop(0, chunks, first, 0)

    def lanes(q):
        return pl.ds(q * QUAD, QUAD)

    def state_copy(q):
        return remote(snd_s.at[q], got_s.at[q], cs.at[q], cr.at[q], ctx + 1, me)

    decay_copy = remote(snd_d, got_d, cs.at[quads], cr.at[quads], ctx + 1, me)

    def enter_copy(q):
        return remote(snd_e.at[q], got_e.at[q], es.at[q], er.at[q], ctx + 2, me)

    def back_copy(q):
        return remote(got_e.at[q], back.at[q], bs.at[q], br.at[q], ctx - 1, me)

    @pl.when(odd == 0)
    def _():
        snd_d[...] = dsum[...]
        decay_copy.start()
        for q in range(quads):
            snd_s[q] = st[:, q * QUAD : (q + 1) * QUAD].astype(BF16)
            state_copy(q).start()

    @pl.when(odd == 1)
    def _():
        decay_copy.wait_recv()

        @pl.when(ctx < 2)
        def _():
            got_e[...] = jnp.zeros_like(got_e)

        for q in range(quads):
            span = slice(q * QUAD, (q + 1) * QUAD)
            state_copy(q).wait_recv()
            mine = jnp.exp(dsum[0:1, span])
            both = jnp.exp(dsum[0:1, span] + got_d[0:1, span])
            pair = mine * got_s[q].astype(F32) + st[:, span]

            @pl.when(ctx >= 2)
            def _():
                enter_copy(q).wait_recv()
                back_copy(q).start()

            entered = got_e[q].astype(F32)

            @pl.when(ctx < places_ctx - 2)
            def _():
                snd_e[q] = (both * entered + pair).astype(BF16)
                enter_copy(q).start()

            inc[:, span] = jnp.exp(got_d[0:1, span]) * entered + got_s[q].astype(F32)

    @pl.when(odd == 0)
    def _():
        @pl.when(ctx < 2)
        def _():
            inc[...] = jnp.zeros_like(inc)

        @pl.when(ctx >= 2)
        def _():
            for q in range(quads):
                back_copy(q).wait_recv()
                inc[:, q * QUAD : (q + 1) * QUAD] = back[q].astype(F32)

    out_load.wait()

    def piece_copy(c):
        return remote(send_p.at[c], recv_p.at[c], rs.at[c], rr.at[c], ctx, partner)

    def far_copy(c):
        return remote(send_y.at[c], recv_y.at[c], zs.at[c], zr.at[c], ctx, other)

    def square_copy(c, h, k, sender):
        return remote(sq.at[sender, c], sq.at[sender, c], qs.at[k, c], qr.at[k, c], ctx, h)

    def columns(h):
        return pl.ds(pl.multiple_of(h * feat, 128), feat)

    def combine(c):
        piece_copy(c).wait_recv()
        own[c, 0] = own[c, 0] + recv_p[c, 0].astype(F32)
        send_y[c] = (own[c, 1] + recv_p[c, 1].astype(F32)).astype(BF16)
        far_copy(c).start()

    def second(c, carry):
        here = pl.ds(pl.multiple_of(c * BLOCK, BLOCK), BLOCK)
        squares = jnp.zeros((BLOCK, 1), F32)
        e_all = ed[here, :]
        cc = cm[here, :]
        for q in range(quads):
            span = slice(q * QUAD, (q + 1) * QUAD)
            carried = ent[c, :, span].astype(F32) + jnp.exp(tl[c, 0:1, span]) * inc[:, span]
            yc = dot(cc, carried.astype(BF16))
            growth = spread(lambda i: e_all[:, i : i + 1], q * PER, lane, BLOCK)
            y = yi[here, span] + growth * yc + skip[:, span] * xc[here, span].astype(F32)
            gated = y * silu(gate[here, span].astype(F32))
            squares = squares + jnp.sum(gated * gated, axis=-1, keepdims=True)
            gb[:, span] = (gated * out_gain[:, span]).astype(BF16)
        g = gb[...]
        send_p[c, 0] = dot(g, wout[:, columns(partner)]).astype(BF16)
        send_p[c, 1] = dot(g, wout[:, columns(diag)]).astype(BF16)
        piece_copy(c).start()
        sq[me, c] = jnp.broadcast_to(squares, (BLOCK, 128)).T[0:8, :]
        for k, h in enumerate((partner, other, diag)):
            square_copy(c, h, k, me).start()
        own[c, 1] = dot(g, wout[:, columns(other)])
        own[c, 0] = dot(g, wout[:, columns(me)])

        @pl.when(c > 0)
        def _():
            combine(c - 1)

        return carry

    lax.fori_loop(0, chunks, second, 0)
    combine(chunks - 1)

    def third(c, carry):
        here = pl.ds(pl.multiple_of(c * BLOCK, BLOCK), BLOCK)
        for k, h in enumerate((partner, other, diag)):
            square_copy(c, h, k, h).wait_recv()
        total = (sq[0, c] + sq[1, c]) + (sq[2, c] + sq[3, c])
        scale_row = lax.rsqrt(total / (4 * inner) + eps)
        scale = jnp.broadcast_to(scale_row[0:1, :], (128, BLOCK)).T[:, 0:1]
        far_copy(c).wait_recv()
        out[here, :] = ((own[c, 0] + recv_y[c].astype(F32)) * scale).astype(BF16)
        return carry

    lax.fori_loop(0, chunks, third, 0)

    for c in range(chunks):
        to_y(c).wait_send()
        to_p(c).wait_send()
        forward(c).wait_send()
        piece_copy(c).wait_send()
        far_copy(c).wait_send()
        for k, h in enumerate((partner, other, diag)):
            square_copy(c, h, k, me).wait_send()

    @pl.when(ctx < places_ctx - 1)
    def _():
        for h in range(4):
            halo(h, me).wait_send()

    @pl.when(odd == 0)
    def _():
        decay_copy.wait_send()
        for q in range(quads):
            state_copy(q).wait_send()

    @pl.when(odd == 1)
    def _():
        @pl.when(ctx >= 2)
        def _():
            for q in range(quads):
                back_copy(q).wait_send()

        @pl.when(ctx < places_ctx - 2)
        def _():
            for q in range(quads):
                enter_copy(q).wait_send()


def per_device(
    places,
    hidden,
    norm_gain,
    zx_weight,
    bc_weight,
    dt_weight,
    conv_x,
    conv_bc,
    dt_bias,
    log_decay,
    skip_gain,
    out_gain,
    out_weight,
):
    rows, feat = hidden.shape
    width = zx_weight.shape[0]
    inner = zx_weight.shape[2]
    heads = dt_weight.shape[1]
    quads = inner // QUAD
    chunks = rows // BLOCK
    any_spec = pl.BlockSpec(memory_space=pl.ANY)
    vmem = pl.BlockSpec(memory_space=pltpu.VMEM)
    dma = pltpu.SemaphoreType.DMA
    return pl.pallas_call(
        functools.partial(kernel, places),
        out_shape=jax.ShapeDtypeStruct((rows, feat), BF16),
        in_specs=[any_spec] * 4 + [vmem] * 8,
        out_specs=vmem,
        scratch_shapes=[
            pltpu.VMEM((4, HALO + rows, feat), BF16),
            pltpu.VMEM((width, 2 * inner), BF16),
            pltpu.VMEM((width, 2 * STATE), BF16),
            pltpu.VMEM((inner, width), BF16),
            pltpu.VMEM((width, 128), BF16),
            pltpu.VMEM((BLOCK, width), BF16),
            pltpu.VMEM((HALO, inner + 2 * STATE), F32),
            pltpu.VMEM((BLOCK, 128), F32),
            pltpu.VMEM((rows, inner), BF16),
            pltpu.VMEM((rows, inner), BF16),
            pltpu.VMEM((rows, STATE), BF16),
            pltpu.VMEM((rows, inner), F32),
            pltpu.VMEM((chunks, STATE, inner), BF16),
            pltpu.VMEM((chunks, 8, inner), F32),
            pltpu.VMEM((rows, 128), F32),
            pltpu.VMEM((STATE, inner), F32),
            pltpu.VMEM((8, inner), F32),
            pltpu.VMEM((quads, STATE, QUAD), BF16),
            pltpu.VMEM((8, inner), F32),
            pltpu.VMEM((quads, STATE, QUAD), BF16),
            pltpu.VMEM((8, inner), F32),
            pltpu.VMEM((quads, STATE, QUAD), BF16),
            pltpu.VMEM((quads, STATE, QUAD), BF16),
            pltpu.VMEM((quads, STATE, QUAD), BF16),
            pltpu.VMEM((STATE, inner), F32),
            pltpu.VMEM((BLOCK, inner), BF16),
            pltpu.VMEM((chunks, 2, BLOCK, feat), BF16),
            pltpu.VMEM((chunks, 2, BLOCK, feat), BF16),
            pltpu.VMEM((chunks, 2, BLOCK, feat), F32),
            pltpu.VMEM((chunks, BLOCK, feat), BF16),
            pltpu.VMEM((chunks, BLOCK, feat), BF16),
            pltpu.VMEM((4, chunks, 8, BLOCK), F32),
            dma((4,)),
            dma((chunks,)),
            dma((chunks,)),
            dma((chunks,)),
            dma((chunks,)),
            dma((chunks,)),
            dma((chunks,)),
            dma((4,)),
            dma((4,)),
            dma((quads + 1,)),
            dma((quads + 1,)),
            dma((quads,)),
            dma((quads,)),
            dma((quads,)),
            dma((quads,)),
            dma((chunks,)),
            dma((chunks,)),
            dma((chunks,)),
            dma((chunks,)),
            dma((3, chunks)),
            dma((3, chunks)),
        ],
        compiler_params=pltpu.CompilerParams(
            collective_id=0, has_side_effects=True, vmem_limit_bytes=63000000
        ),
        name="mixer",
    )(
        hidden,
        zx_weight.reshape(width, 2 * inner),
        bc_weight,
        out_weight,
        norm_gain.reshape(1, width),
        dt_weight,
        conv_x,
        conv_bc,
        jnp.pad(dt_bias, (0, 128 - heads)).reshape(1, 128),
        log_decay,
        jnp.repeat(skip_gain, HEADDIM).reshape(1, inner),
        out_gain.reshape(1, inner),
    )


def solution(mesh):
    placed = (
        P("ctx", "head"),
        P(),
        P(None, None, "head"),
        P(),
        P(None, "head"),
        P(None, "head"),
        P(),
        P("head"),
        P("ctx", "head"),
        P("head"),
        P("head"),
        P("head", None),
    )
    return jax.shard_map(
        functools.partial(per_device, mesh.shape["ctx"]),
        mesh=mesh,
        in_specs=placed,
        out_specs=P("ctx", "head"),
        check_vma=False,
    )
```

time: 210 us -> 91 us (0.43)
  waiting for transfers between devices: 87.4 us -> 0 us
  Pallas kernels: 0 us -> 74.3 us
  matrix products: 28.3 us -> 0 us
  other arithmetic: 21.4 us -> 0 us
  blocking collectives: 20.7 us -> 0 us
  between operations: 14.1 us -> 0.01 us
  local copies, waits for them, and re-layouts: 30 us -> 16.3 us
  starting transfers between devices: 5.62 us -> 0 us
    pallas_call x0 -> x1, Pallas kernels: none -> 74.3 us  [per_device(): pl.pallas_call(functools.partial(kernel, places), out_shape=jax.ShapeDtyp...]
    all_gather x2 -> x0, waiting for transfers between devices: 44.4 us -> none  [the longest x1 22.5 us: carried_in(): lax.all_gather(a.astype(kind), axis)]
    unnamed x4 -> x0, waiting for transfers between devices: 39.8 us -> none
    dot_general x8 -> x0, matrix products: 28.3 us -> none  [the longest x1 7.83 us: project_rows(): jnp.dot(normed, flat_weight, preferred_element_type=jnp.float32)]
    unnamed x1 -> x0, blocking collectives: 14.6 us -> none
    reduce_sum x3 -> x0, other arithmetic: 6.46 us -> none  [the longest x1 3.49 us: per_device(): square_sum = lax.psum(jnp.sum(gated * gated, axis=-1), 'head')]
    add x6 -> x0, other arithmetic: 6.4 us -> none  [combine(): jnp.exp(later_pair[0])[:, None, None] * earlier_pair[1] + later_pair[1]]
    psum x1 -> x0, blocking collectives: 6.04 us -> none  [per_device(): square_sum = lax.psum(jnp.sum(gated * gated, axis=-1), 'head')]
  transfers between devices with their start and end apart: 5 -> 0, of which waited for: 4 -> 0; matrix products, arithmetic and copies ran while one was open for 8% -> 0% of each run, Pallas kernels for 0% -> 0%
where the time goes in v1:
time: 91 us; the launch traced here: 90.6 us
  Pallas kernels  74.3 us (82%)
  local copies, waits for them, and re-layouts  16.3 us (18%)
    pallas_call x1, Pallas kernels, per_device(): pl.pallas_call(functools.partial(kernel, places), out_shape=jax.ShapeDtyp...  74.3 us
    unnamed x4, local copies, waits for them, and re-layouts  11.1 us

profile of v1, /device:TPU:24, one launch (start us, length us, event | category | flops | bytes accessed | tf_op | source)
XLA Modules:
  0.0 90.6 jit_solution(9502736445828294696)
XLA Ops:
  0.0 1.2 %pad_bitcast_fusion.dtb = f32[1,128]{1,0:T(1,128)} fusion(f32[12]{0:T(128)} %param.19), kind=kLoop, calls=%fused_computation | loop fusion | bytes 560 | tf_op jit(solution)/shard_map/reshape | solution.py:569
  1.2 1.3 %reshape.15.out_gain = f32[1,768]{1,0:T(1,128)} reshape(f32[768]{0:T(1024)} %param.22) | data formatting | bytes 6144 | tf_op jit(solution)/shard_map/reshape | solution.py:572
  2.5 1.3 %reshape.13.gain = f32[1,1536]{1,0:T(1,128)} reshape(f32[1536]{0:T(1024)} %param.13) | data formatting | bytes 12288 | tf_op jit(solution)/shard_map/reshape | solution.py:565
  3.8 0.7 broadcast_in_dim.3
  4.5 0.7 reshape_reshape.3.skip
  5.2 1.8 %copy.13.wdt_in = bf16[1536,12]{1,0:T(8,128)(2,1)} copy(bf16[1536,12]{0,1:T(8,128)(2,1)} %param.16) | data formatting | bytes 73728 | tf_op args[4]
  6.9 1.9 %copy.14.ld_in = f32[1024,12]{1,0:T(8,128)} copy(f32[1024,12]{0,1:T(8,128)} %param.20) | data formatting | bytes 98304 | tf_op args[8]
  8.8 5.4 %copy.15 = bf16[192,8,2,768]{3,1,2,0:T(8,128)(2,1)} copy(bf16[192,8,2,768]{3,2,1,0:T(2,128)(2,1)} %bitcast.5) | data formatting | bytes 9437184
  14.2 74.3 %mixer.1 = bf16[1024,384]{1,0:T(8,128)(2,1)} custom-call(bf16[1024,384]{1,0:T(8,128)(2,1)} %hidden.1, bf16[1536,1536]{1,0:T(8,128)(2,1)} %bitcast.4, bf16[1536,256]{1,0:T(8,128)(2,1)} %wbc_hbm.1, bf16[768,1536]{1,0:T(8,128)(2,1)} %wout_hbm.1, f32[1,1536]{1,0:T(1,128)} %reshape.13.gain, bf16[1536,12]{1,0:T(8,128)(2,1)} %copy.13.wdt_in, f32[5,768]{1,0:T(8,128)} %taps_x.1, ...), custom_call_target="tpu_custom_call" | custom-call | tf_op jit(solution)/shard_map/mixer/pallas_call | solution.py:496
  88.5 2.1 %copy.17 = bf16[1024,384]{1,0:T(8,128)(2,1)} copy(bf16[1024,384]{1,0:T(8,128)(2,1)} %mixer.1) | data formatting | bytes 1572864

commit v2 on v1

--- a/solution.py
+++ b/solution.py
@@ -52,10 +52,13 @@
     out_gain,
     out,
     xg,
+    wraw,
     wzx,
     wbc,
     wout,
     wdt,
+    dtrow,
+    skrow,
     nrm,
     tail,
     ldp,
@@ -128,7 +131,7 @@
     own_load = pltpu.make_async_copy(hidden, xg.at[me, pl.ds(HALO, rows)], load_sem.at[0])
     loads = [
         pltpu.make_async_copy(wbc_hbm, wbc, load_sem.at[1]),
-        pltpu.make_async_copy(wzx_hbm, wzx, load_sem.at[2]),
+        pltpu.make_async_copy(wzx_hbm, wraw, load_sem.at[2]),
     ]
     out_load = pltpu.make_async_copy(wout_hbm, wout, load_sem.at[3])
 
@@ -207,8 +210,20 @@
     def _():
         xg[:, 0:HALO, :] = jnp.zeros((4, HALO, feat), BF16)
 
-    wdt[...] = jnp.zeros_like(wdt)
-    wdt[:, 0:heads] = wdt_in[...]
+    dt_wide = jnp.concatenate(
+        [wdt_in[...].astype(F32), jnp.zeros((128 - heads, width), F32)], axis=0
+    )
+    wdt[...] = dt_wide.T.astype(BF16)
+    few = lax.broadcasted_iota(jnp.int32, (8, 128), 1)
+    bias_row = jnp.zeros((8, 128), F32)
+    for h in range(heads):
+        bias_row = jnp.where(few == h, dtb[h], bias_row)
+    dtrow[...] = bias_row
+    wide = lax.broadcasted_iota(jnp.int32, (8, inner), 1)
+    skip_row = jnp.zeros((8, inner), F32)
+    for h in range(heads):
+        skip_row = jnp.where(wide >= h * HEADDIM, skip[h], skip_row)
+    skrow[...] = skip_row
     ldp[...] = jnp.zeros_like(ldp)
     st[...] = jnp.zeros_like(st)
     dsum[...] = jnp.zeros_like(dsum)
@@ -221,6 +236,15 @@
     for load in loads:
         load.wait()
     own_load.wait()
+
+    def split(i, carry):
+        at = pl.ds(pl.multiple_of(i * 64, 64), 64)
+        both = wraw[at, :, :]
+        wzx[at, 0:inner] = both[:, 0, :]
+        wzx[at, inner : 2 * inner] = both[:, 1, :]
+        return carry
+
+    lax.fori_loop(0, width // 64, split, 0)
 
     def normalised(at, count):
         vals = [xg[j, at, :].astype(F32) for j in range(4)]
@@ -228,7 +252,7 @@
         scale = lax.rsqrt(total / width + eps)
         for j in range(4):
             span = slice(j * feat, (j + 1) * feat)
-            nrm[0:count, span] = (vals[j] * scale * gain[:, span]).astype(BF16)
+            nrm[0:count, span] = (vals[j] * scale * gain[span].reshape(1, feat)).astype(BF16)
 
     normalised(pl.ds(0, HALO), HALO)
     head_rows = nrm[0:HALO, :]
@@ -263,13 +287,13 @@
         b = bc[:, :STATE].astype(BF16)
         cc = bc[:, STATE:].astype(BF16)
         cm[here, :] = cc
-        raw_step = dot(normed, wdt[...]) + dtb[...]
+        raw_step = dot(normed, wdt[...]) + dtrow[0:1, :]
         step = jnp.maximum(raw_step, 0.0) + jnp.log1p(jnp.exp(-jnp.abs(raw_step)))
-        ldp[:, 0:heads] = ld_in[here, :]
-        tri = jnp.where(row_id >= col_id, 1.0, 0.0).astype(F32)
-        dcol = jnp.dot(tri, ldp[...], preferred_element_type=F32, precision=lax.Precision.HIGHEST)
+        ldp[0:heads, :] = ld_in[:, here]
+        tri = jnp.where(row_id <= col_id, 1.0, 0.0).astype(F32)
+        drow = jnp.dot(ldp[...], tri, preferred_element_type=F32, precision=lax.Precision.HIGHEST)
+        dcol = drow.T
         ed[here, :] = jnp.exp(dcol)
-        drow = dcol.T
         srow = step.T
         wrow = jnp.exp(drow[:, BLOCK - 1 : BLOCK] - drow) * srow
         scores = lax.dot_general(
@@ -400,10 +424,10 @@
             carried = ent[c, :, span].astype(F32) + jnp.exp(tl[c, 0:1, span]) * inc[:, span]
             yc = dot(cc, carried.astype(BF16))
             growth = spread(lambda i: e_all[:, i : i + 1], q * PER, lane, BLOCK)
-            y = yi[here, span] + growth * yc + skip[:, span] * xc[here, span].astype(F32)
+            y = yi[here, span] + growth * yc + skrow[0:1, span] * xc[here, span].astype(F32)
             gated = y * silu(gate[here, span].astype(F32))
             squares = squares + jnp.sum(gated * gated, axis=-1, keepdims=True)
-            gb[:, span] = (gated * out_gain[:, span]).astype(BF16)
+            gb[:, span] = (gated * out_gain[span].reshape(1, QUAD)).astype(BF16)
         g = gb[...]
         send_p[c, 0] = dot(g, wout[:, columns(partner)]).astype(BF16)
         send_p[c, 1] = dot(g, wout[:, columns(diag)]).astype(BF16)
@@ -492,21 +516,25 @@
     chunks = rows // BLOCK
     any_spec = pl.BlockSpec(memory_space=pl.ANY)
     vmem = pl.BlockSpec(memory_space=pltpu.VMEM)
+    smem = pl.BlockSpec(memory_space=pltpu.SMEM)
     dma = pltpu.SemaphoreType.DMA
     return pl.pallas_call(
         functools.partial(kernel, places),
         out_shape=jax.ShapeDtypeStruct((rows, feat), BF16),
-        in_specs=[any_spec] * 4 + [vmem] * 8,
+        in_specs=[any_spec] * 4 + [vmem] * 4 + [smem, vmem, smem, vmem],
         out_specs=vmem,
         scratch_shapes=[
             pltpu.VMEM((4, HALO + rows, feat), BF16),
+            pltpu.VMEM((width, 2, inner), BF16),
             pltpu.VMEM((width, 2 * inner), BF16),
             pltpu.VMEM((width, 2 * STATE), BF16),
             pltpu.VMEM((inner, width), BF16),
             pltpu.VMEM((width, 128), BF16),
+            pltpu.VMEM((8, 128), F32),
+            pltpu.VMEM((8, inner), F32),
             pltpu.VMEM((BLOCK, width), BF16),
             pltpu.VMEM((HALO, inner + 2 * STATE), F32),
-            pltpu.VMEM((BLOCK, 128), F32),
+            pltpu.VMEM((128, BLOCK), F32),
             pltpu.VMEM((rows, inner), BF16),
             pltpu.VMEM((rows, inner), BF16),
             pltpu.VMEM((rows, STATE), BF16),
@@ -559,17 +587,17 @@
         name="mixer",
     )(
         hidden,
-        zx_weight.reshape(width, 2 * inner),
+        zx_weight,
         bc_weight,
         out_weight,
-        norm_gain.reshape(1, width),
-        dt_weight,
+        norm_gain,
+        dt_weight.T,
         conv_x,
         conv_bc,
-        jnp.pad(dt_bias, (0, 128 - heads)).reshape(1, 128),
-        log_decay,
-        jnp.repeat(skip_gain, HEADDIM).reshape(1, inner),
-        out_gain.reshape(1, inner),
+        dt_bias,
+        log_decay.T,
+        skip_gain,
+        out_gain,
     )
 
 

time: 91 us -> 80.9 us (0.89)
  local copies, waits for them, and re-layouts: 16.3 us -> 2.09 us
  Pallas kernels: 74.3 us -> 78.6 us
    unnamed x4 -> x1, local copies, waits for them, and re-layouts: 11.1 us -> 2.09 us
    pallas_call x1, Pallas kernels: 74.3 us -> 78.6 us  [per_device(): pl.pallas_call(functools.partial(kernel, places), out_shape=jax.ShapeDtyp...]
    reshape x3 -> x0, local copies, waits for them, and re-layouts: 3.76 us -> none  [the longest x1 1.3 us: per_device(): norm_gain.reshape(1, width)]
where the time goes in v2:
time: 80.9 us; the launch traced here: 80.7 us
  Pallas kernels  78.6 us (97%)
  local copies, waits for them, and re-layouts  2.09 us (3%)
    pallas_call x1, Pallas kernels, per_device(): pl.pallas_call(functools.partial(kernel, places), out_shape=jax.ShapeDtyp...  78.6 us
    unnamed x1, local copies, waits for them, and re-layouts  2.09 us

profile of v2, /device:TPU:24, one launch (start us, length us, event | category | flops | bytes accessed | tf_op | source)
XLA Modules:
  0.0 80.7 jit_solution(14079711449072575318)
XLA Ops:
  0.0 78.6 %mixer.1 = bf16[1024,384]{1,0:T(8,128)(2,1)} custom-call(bf16[1024,384]{1,0:T(8,128)(2,1)} %hidden.1, bf16[1536,2,768]{2,1,0:T(2,128)(2,1)} %wzx_hbm.1, bf16[1536,256]{1,0:T(8,128)(2,1)} %wbc_hbm.1, bf16[768,1536]{1,0:T(8,128)(2,1)} %wout_hbm.1, f32[1536]{0:T(1024)} %gain.1, bf16[12,1536]{1,0:T(8,128)(2,1)} %bitcast.3, f32[5,768]{1,0:T(8,128)} %taps_x.1, ...), custom_call_target="tpu_custom_call" | custom-call | tf_op jit(solution)/shard_map/mixer/pallas_call | solution.py:521
  78.6 2.1 %copy.14 = bf16[1024,384]{1,0:T(8,128)(2,1)} copy(bf16[1024,384]{1,0:T(8,128)(2,1)} %mixer.1) | data formatting | bytes 1572864

commit v3 on v2

--- a/solution.py
+++ b/solution.py
@@ -13,6 +13,7 @@
 BLOCK = 256
 HALO = 16
 QUAD = 256
+GROUP = 128
 PER = QUAD // HEADDIM
 
 eps = 1e-05
@@ -77,8 +78,13 @@
     snd_d,
     got_e,
     snd_e,
+    snd_b,
     back,
     inc,
+    sc_keep,
+    dc_keep,
+    dr_keep,
+    sr_keep,
     gb,
     send_p,
     recv_p,
@@ -275,7 +281,26 @@
         tail[:, span] = raw[BLOCK - HALO :, :]
         return silu(summed[HALO:, :])
 
+    def inside(c):
+        here = pl.ds(pl.multiple_of(c * BLOCK, BLOCK), BLOCK)
+        scores = sc_keep[...]
+        for q in range(quads):
+            span = slice(q * QUAD, (q + 1) * QUAD)
+            xq = xc[here, span]
+            y_acc = None
+            for k in range(PER):
+                h = q * PER + k
+                gap = jnp.minimum(dc_keep[:, h : h + 1] - dr_keep[h : h + 1, :], 0.0)
+                mix = (scores * jnp.exp(gap) * sr_keep[h : h + 1, :]).astype(BF16)
+                y_h = dot(mix, xq)
+                y_acc = y_h if k == 0 else jnp.where(lane >= k * HEADDIM, y_h, y_acc)
+            yi[here, span] = y_acc
+
     def first(c, carry):
+        @pl.when(c > 0)
+        def _():
+            inside(c - 1)
+
         to_y(c).wait_recv()
         forward(c).start()
         to_p(c).wait_recv()
@@ -299,7 +324,10 @@
         scores = lax.dot_general(
             cc, b, (((1,), (1,)), ((), ())), preferred_element_type=F32
         )
-        scores = jnp.where(row_id >= col_id, scores, 0.0)
+        sc_keep[...] = jnp.where(row_id >= col_id, scores, 0.0)
+        dc_keep[...] = dcol
+        dr_keep[...] = drow[0:16, :]
+        sr_keep[...] = srow[0:16, :]
         b_t = b.astype(F32).T
         for q in range(quads):
             span = slice(q * QUAD, (q + 1) * QUAD)
@@ -307,21 +335,15 @@
             raw = dot(normed, wzx[:, inner + q * QUAD : inner + (q + 1) * QUAD])
             xq = convolved(raw, span, taps_x[:, span]).astype(BF16)
             xc[here, span] = xq
-            y_acc = None
             s_acc = None
             for k in range(PER):
                 h = q * PER + k
-                gap = jnp.minimum(dcol[:, h : h + 1] - drow[h : h + 1, :], 0.0)
-                mix = (scores * jnp.exp(gap) * srow[h : h + 1, :]).astype(BF16)
                 wb = (b_t * wrow[h : h + 1, :]).astype(BF16)
-                y_h = dot(mix, xq)
                 s_h = dot(wb, xq)
                 if k == 0:
-                    y_acc, s_acc = y_h, s_h
+                    s_acc = s_h
                 else:
-                    y_acc = jnp.where(lane >= k * HEADDIM, y_h, y_acc)
                     s_acc = jnp.where(lane >= k * HEADDIM, s_h, s_acc)
-            yi[here, span] = y_acc
             total = spread(lambda i: dcol[BLOCK - 1 : BLOCK, i : i + 1], q * PER, lane, 1)
             ent[c, :, span] = st[:, span].astype(BF16)
             tl[c, :, span] = dsum[:, span]
@@ -331,68 +353,87 @@
 
     lax.fori_loop(0, chunks, first, 0)
 
-    def lanes(q):
-        return pl.ds(q * QUAD, QUAD)
-
-    def state_copy(q):
-        return remote(snd_s.at[q], got_s.at[q], cs.at[q], cr.at[q], ctx + 1, me)
-
-    decay_copy = remote(snd_d, got_d, cs.at[quads], cr.at[quads], ctx + 1, me)
-
-    def enter_copy(q):
-        return remote(snd_e.at[q], got_e.at[q], es.at[q], er.at[q], ctx + 2, me)
-
-    def back_copy(q):
-        return remote(got_e.at[q], back.at[q], bs.at[q], br.at[q], ctx - 1, me)
-
-    @pl.when(odd == 0)
-    def _():
+    groups = inner // GROUP
+
+    def part(g):
+        return slice(g * GROUP, (g + 1) * GROUP)
+
+    def state_copy(g, c):
+        return remote(snd_s.at[g], got_s.at[g], cs.at[g], cr.at[g], c, me)
+
+    def decay_copy(c):
+        return remote(snd_d, got_d, cs.at[groups], cr.at[groups], c, me)
+
+    def enter_copy(g):
+        return remote(snd_e.at[g], got_e.at[g], es.at[g], er.at[g], ctx + 2, me)
+
+    def back_copy(g, c):
+        return remote(snd_b.at[g], back.at[g], bs.at[g], br.at[g], c, me)
+
+    even_led = [g for g in range(groups) if g % 2 == 0]
+    odd_led = [g for g in range(groups) if g % 2 == 1]
+
+    def pair_scan(is_odd, mate, led, followed):
         snd_d[...] = dsum[...]
-        decay_copy.start()
-        for q in range(quads):
-            snd_s[q] = st[:, q * QUAD : (q + 1) * QUAD].astype(BF16)
-            state_copy(q).start()
-
-    @pl.when(odd == 1)
-    def _():
-        decay_copy.wait_recv()
-
-        @pl.when(ctx < 2)
-        def _():
-            got_e[...] = jnp.zeros_like(got_e)
-
-        for q in range(quads):
-            span = slice(q * QUAD, (q + 1) * QUAD)
-            state_copy(q).wait_recv()
-            mine = jnp.exp(dsum[0:1, span])
-            both = jnp.exp(dsum[0:1, span] + got_d[0:1, span])
-            pair = mine * got_s[q].astype(F32) + st[:, span]
+        decay_copy(mate).start()
+        for g in followed:
+            snd_s[g] = st[:, part(g)].astype(BF16)
+            state_copy(g, mate).start()
+        inside(chunks - 1)
+        decay_copy(mate).wait_recv()
+        for g in led:
+            at = part(g)
+            state_copy(g, mate).wait_recv()
+            mine = dsum[0:1, at]
+            theirs = got_d[0:1, at]
+            if is_odd:
+                pair = jnp.exp(mine) * got_s[g].astype(F32) + st[:, at]
+            else:
+                pair = jnp.exp(theirs) * st[:, at] + got_s[g].astype(F32)
 
             @pl.when(ctx >= 2)
             def _():
-                enter_copy(q).wait_recv()
-                back_copy(q).start()
-
-            entered = got_e[q].astype(F32)
+                enter_copy(g).wait_recv()
+
+            entered = got_e[g].astype(F32)
 
             @pl.when(ctx < places_ctx - 2)
             def _():
-                snd_e[q] = (both * entered + pair).astype(BF16)
-                enter_copy(q).start()
-
-            inc[:, span] = jnp.exp(got_d[0:1, span]) * entered + got_s[q].astype(F32)
+                snd_e[g] = (jnp.exp(mine + theirs) * entered + pair).astype(BF16)
+                enter_copy(g).start()
+
+            if is_odd:
+                snd_b[g] = got_e[g]
+                inc[:, at] = jnp.exp(theirs) * entered + got_s[g].astype(F32)
+            else:
+                snd_b[g] = (jnp.exp(mine) * entered + st[:, at]).astype(BF16)
+                inc[:, at] = entered
+            back_copy(g, mate).start()
+        for g in followed:
+            back_copy(g, mate).wait_recv()
+            inc[:, part(g)] = back[g].astype(F32)
+        decay_copy(mate).wait_send()
+        for g in followed:
+            state_copy(g, mate).wait_send()
+        for g in led:
+            back_copy(g, mate).wait_send()
+
+        @pl.when(ctx < places_ctx - 2)
+        def _():
+            for g in led:
+                enter_copy(g).wait_send()
+
+    @pl.when(ctx < 2)
+    def _():
+        got_e[...] = jnp.zeros_like(got_e)
 
     @pl.when(odd == 0)
     def _():
-        @pl.when(ctx < 2)
-        def _():
-            inc[...] = jnp.zeros_like(inc)
-
-        @pl.when(ctx >= 2)
-        def _():
-            for q in range(quads):
-                back_copy(q).wait_recv()
-                inc[:, q * QUAD : (q + 1) * QUAD] = back[q].astype(F32)
+        pair_scan(0, ctx + 1, even_led, odd_led)
+
+    @pl.when(odd == 1)
+    def _():
+        pair_scan(1, ctx - 1, odd_led, even_led)
 
     out_load.wait()
 
@@ -474,24 +515,6 @@
         for h in range(4):
             halo(h, me).wait_send()
 
-    @pl.when(odd == 0)
-    def _():
-        decay_copy.wait_send()
-        for q in range(quads):
-            state_copy(q).wait_send()
-
-    @pl.when(odd == 1)
-    def _():
-        @pl.when(ctx >= 2)
-        def _():
-            for q in range(quads):
-                back_copy(q).wait_send()
-
-        @pl.when(ctx < places_ctx - 2)
-        def _():
-            for q in range(quads):
-                enter_copy(q).wait_send()
-
 
 def per_device(
     places,
@@ -512,7 +535,7 @@
     width = zx_weight.shape[0]
     inner = zx_weight.shape[2]
     heads = dt_weight.shape[1]
-    quads = inner // QUAD
+    groups = inner // GROUP
     chunks = rows // BLOCK
     any_spec = pl.BlockSpec(memory_space=pl.ANY)
     vmem = pl.BlockSpec(memory_space=pltpu.VMEM)
@@ -544,14 +567,19 @@
             pltpu.VMEM((rows, 128), F32),
             pltpu.VMEM((STATE, inner), F32),
             pltpu.VMEM((8, inner), F32),
-            pltpu.VMEM((quads, STATE, QUAD), BF16),
+            pltpu.VMEM((groups, STATE, GROUP), BF16),
             pltpu.VMEM((8, inner), F32),
-            pltpu.VMEM((quads, STATE, QUAD), BF16),
+            pltpu.VMEM((groups, STATE, GROUP), BF16),
             pltpu.VMEM((8, inner), F32),
-            pltpu.VMEM((quads, STATE, QUAD), BF16),
-            pltpu.VMEM((quads, STATE, QUAD), BF16),
-            pltpu.VMEM((quads, STATE, QUAD), BF16),
+            pltpu.VMEM((groups, STATE, GROUP), BF16),
+            pltpu.VMEM((groups, STATE, GROUP), BF16),
+            pltpu.VMEM((groups, STATE, GROUP), BF16),
+            pltpu.VMEM((groups, STATE, GROUP), BF16),
             pltpu.VMEM((STATE, inner), F32),
+            pltpu.VMEM((BLOCK, BLOCK), F32),
+            pltpu.VMEM((BLOCK, 128), F32),
+            pltpu.VMEM((16, BLOCK), F32),
+            pltpu.VMEM((16, BLOCK), F32),
             pltpu.VMEM((BLOCK, inner), BF16),
             pltpu.VMEM((chunks, 2, BLOCK, feat), BF16),
             pltpu.VMEM((chunks, 2, BLOCK, feat), BF16),
@@ -568,12 +596,12 @@
             dma((chunks,)),
             dma((4,)),
             dma((4,)),
-            dma((quads + 1,)),
-            dma((quads + 1,)),
-            dma((quads,)),
-            dma((quads,)),
-            dma((quads,)),
-            dma((quads,)),
+            dma((groups + 1,)),
+            dma((groups + 1,)),
+            dma((groups,)),
+            dma((groups,)),
+            dma((groups,)),
+            dma((groups,)),
             dma((chunks,)),
             dma((chunks,)),
             dma((chunks,)),

time: 80.9 us -> 80.2 us (level); the launches traced: 80.7 us -> 79.1 us
  Pallas kernels: 78.6 us -> 77 us
    pallas_call x1, Pallas kernels: 78.6 us -> 77 us  [per_device(): pl.pallas_call(functools.partial(kernel, places), out_shape=jax.ShapeDtyp...]
where the time goes in v3:
time: 80.2 us; the launch traced here: 79.1 us
  Pallas kernels  77 us (96%)
  local copies, waits for them, and re-layouts  2.09 us (3%)
    pallas_call x1, Pallas kernels, per_device(): pl.pallas_call(functools.partial(kernel, places), out_shape=jax.ShapeDtyp...  77 us
    unnamed x1, local copies, waits for them, and re-layouts  2.09 us

profile of v3, /device:TPU:24, one launch (start us, length us, event | category | flops | bytes accessed | tf_op | source)
XLA Modules:
  0.0 79.1 jit_solution(17748942518250675754)
XLA Ops:
  0.0 77.0 %mixer.1 = bf16[1024,384]{1,0:T(8,128)(2,1)} custom-call(bf16[1024,384]{1,0:T(8,128)(2,1)} %hidden.1, bf16[1536,2,768]{2,1,0:T(2,128)(2,1)} %wzx_hbm.1, bf16[1536,256]{1,0:T(8,128)(2,1)} %wbc_hbm.1, bf16[768,1536]{1,0:T(8,128)(2,1)} %wout_hbm.1, f32[1536]{0:T(1024)} %gain.1, bf16[12,1536]{1,0:T(8,128)(2,1)} %bitcast.3, f32[5,768]{1,0:T(8,128)} %taps_x.1, ...), custom_call_target="tpu_custom_call" | custom-call | tf_op jit(solution)/shard_map/mixer/pallas_call | solution.py:544
  77.0 2.1 %copy.14 = bf16[1024,384]{1,0:T(8,128)(2,1)} copy(bf16[1024,384]{1,0:T(8,128)(2,1)} %mixer.1) | data formatting | bytes 1572864
